TPU v7x, 32 devices: a whole 2x2x4 slice. The times are simulated.
32 devices in a mesh: dp: 8 (over y, x, core), tensor: 4 (over z).
Axes of the slice: x: 2, y: 2, z: 4, core: 2. Of those that a mesh axis runs over, the one named last changes fastest.
Arguments:
- tokens: bfloat16 [4096, 768], P('dp'), may hold values from -6 to 6
- lengths: int32 [8, 16], P('dp'), may hold values from 0 to 512, as said below
- w_query: bfloat16 [768, 768], P(None, 'tensor'), may hold values from -0.21875 to 0.21875
- w_key: bfloat16 [768, 768], P(None, 'tensor'), may hold values from -0.21875 to 0.21875
- w_value: bfloat16 [768, 768], P(None, 'tensor'), may hold values from -0.21875 to 0.21875
- b_query: float32 [768], P('tensor'), may hold values from -3 to 3
- b_value: float32 [768], P('tensor'), may hold values from -3 to 3
- w_out: bfloat16 [768, 768], P('tensor'), may hold values from -0.625 to 0.625
- b_out: float32 [768], replicated, may hold values from -3 to 3
- g_attn: float32 [768], replicated, may hold values from 0.5 to 1.5
- b_attn: float32 [768], replicated, may hold values from -3 to 3
- w_up: bfloat16 [768, 3072], P(None, 'tensor'), may hold values from -0.21875 to 0.21875
- b_up: float32 [3072], P('tensor'), may hold values from -3 to 3
- w_down: bfloat16 [3072, 768], P('tensor'), may hold values from -0.109375 to 0.109375
- b_down: float32 [768], replicated, may hold values from -3 to 3
- g_ffn: float32 [768], replicated, may hold values from 0.5 to 1.5
- b_ffn: float32 [768], replicated, may hold values from -3 to 3
- out_grad: bfloat16 [4096, 768], P('dp'), may hold values from -6 to 6
- pool_grad: float32 [128, 1728], P('dp'), may hold values from -6 to 6
Outputs:
- layer_out: bfloat16 [4096, 768], P('dp')
- pools: float32 [128, 1728], replicated
- d_tokens: float32 [4096, 768], P('dp')
- d_w_query: float32 [768, 768], P(None, 'tensor')
- d_w_key: float32 [768, 768], P(None, 'tensor')
- d_w_value: float32 [768, 768], P(None, 'tensor')
- d_b_query: float32 [768], P('tensor')
- d_b_value: float32 [768], P('tensor')
- d_w_out: float32 [768, 768], P('tensor')
- d_b_out: float32 [768], replicated
- d_g_attn: float32 [768], replicated
- d_b_attn: float32 [768], replicated
- d_w_up: float32 [768, 3072], P(None, 'tensor')
- d_b_up: float32 [3072], P('tensor')
- d_w_down: float32 [3072, 768], P('tensor')
- d_b_down: float32 [768], replicated
- d_g_ffn: float32 [768], replicated
- d_b_ffn: float32 [768], replicated
Inputs may be any that keep to these rules, and one draw needn't show every extreme that they name: In each bucket the nonzero lengths come first and add up to at most 512; the first is nonzero; in every draw some bucket holds one sentence of exactly 512 tokens.
All inputs are finite; a program needn't handle non-finite values.
Results may differ from a plain program's by a relative error of at most 0.013.
Values sent between devices are 32-bit elements; how exact they have to be, the bound alone decides.
No kernel may reach another device: no remote copies, remote signals or barrier semaphores. Data moves between devices by JAX's collectives and lax.ppermute only.
A program may use at most 128 MiB of HBM per device.

v0:
```python
import jax
import jax.numpy as jnp
from jax import lax
from jax.sharding import PartitionSpec as P

HDIM = 64
SENTS = 16
norm_eps = 1e-06
pool_eps = 1e-05
highest = lax.Precision.HIGHEST


def truncations(width):
    return [width, width * 2 // 3, width // 3, width // 6, width // 12]


def segment_ids(sizes, slot_count):
    ends = jnp.cumsum(sizes, dtype=jnp.int32)
    places = jnp.arange(slot_count, dtype=jnp.int32)
    return jnp.sum((places[:, None] >= ends[None, :]).astype(jnp.int32), axis=1)


def norm_stats(rows):
    centre = jnp.mean(rows, axis=-1, keepdims=True)
    shifted = rows - centre
    inverse = lax.rsqrt(jnp.mean(shifted * shifted, axis=-1, keepdims=True) + norm_eps)
    return (shifted * inverse, inverse)


def norm_back(grad_in, normal, inverse):
    centre = jnp.mean(grad_in, axis=-1, keepdims=True)
    along = jnp.mean(grad_in * normal, axis=-1, keepdims=True)
    return inverse * (grad_in - centre - normal * along)


def gelu_exact(upper):
    return jax.nn.gelu(upper, approximate=False)


def attention_scores(query_heads, key_heads, allowed, score_scale):
    scores = (
        jnp.einsum("qhd,khd->hqk", query_heads, key_heads, preferred_element_type=jnp.float32)
        * score_scale
    )
    return jnp.where(allowed[None], scores, -1000000000.0)


def shards(
    tokens,
    lengths,
    w_query,
    w_key,
    w_value,
    b_query,
    b_value,
    w_out,
    b_out,
    g_attn,
    b_attn,
    w_up,
    b_up,
    w_down,
    b_down,
    g_ffn,
    b_ffn,
    out_grad,
    pool_grad,
):
    slot_count = tokens.shape[0]
    model_width = tokens.shape[1]
    local_cols = w_query.shape[1]
    head_count = local_cols // HDIM
    score_scale = HDIM ** (-0.5)
    segment = segment_ids(lengths[0], slot_count)
    allowed = segment[:, None] == segment[None, :]
    inputs = tokens.astype(jnp.float32)
    query_rows = (jnp.dot(tokens, w_query, preferred_element_type=jnp.float32) + b_query).astype(
        jnp.bfloat16
    )
    key_rows = jnp.dot(tokens, w_key, preferred_element_type=jnp.float32).astype(jnp.bfloat16)
    value_rows = (jnp.dot(tokens, w_value, preferred_element_type=jnp.float32) + b_value).astype(
        jnp.bfloat16
    )
    query_heads = query_rows.reshape(slot_count, head_count, HDIM)
    key_heads = key_rows.reshape(slot_count, head_count, HDIM)
    value_heads = value_rows.reshape(slot_count, head_count, HDIM)
    scores = attention_scores(query_heads, key_heads, allowed, score_scale)
    top_score = jnp.max(scores, axis=-1, keepdims=True)
    log_total = top_score + jnp.log(jnp.sum(jnp.exp(scores - top_score), axis=-1, keepdims=True))
    probs_low = jnp.exp(scores - log_total).astype(jnp.bfloat16)
    mixed = jnp.einsum("hqk,khd->qhd", probs_low, value_heads, preferred_element_type=jnp.float32)
    mixed = mixed.reshape(slot_count, local_cols).astype(jnp.bfloat16)
    partial_value = jnp.dot(mixed, w_out, preferred_element_type=jnp.float32)
    attn_total = lax.psum(partial_value, "tensor")
    normal_attn, inverse_attn = norm_stats(inputs + attn_total + b_out)
    normed = normal_attn * g_attn + b_attn
    normed_low = normed.astype(jnp.bfloat16)
    upper = jnp.dot(normed_low, w_up, preferred_element_type=jnp.float32) + b_up
    act_rows = gelu_exact(upper).astype(jnp.bfloat16)
    down_total = lax.psum(jnp.dot(act_rows, w_down, preferred_element_type=jnp.float32), "tensor")
    normal_ffn, inverse_ffn = norm_stats(normed + down_total + b_down)
    final = normal_ffn * g_ffn + b_ffn
    layer_out = final.astype(jnp.bfloat16)
    sentence = jnp.arange(SENTS, dtype=jnp.int32)
    member = (segment[None, :] == sentence[:, None]).astype(jnp.float32)
    denom = jnp.maximum(lengths[0], 1).astype(jnp.float32)[:, None]
    pooled = jnp.dot(member, final, precision=highest, preferred_element_type=jnp.float32) / denom
    pieces = []
    factors = []
    for keep_width in truncations(model_width):
        leading = pooled[:, :keep_width]
        factor = lax.rsqrt(jnp.mean(leading * leading, axis=1, keepdims=True) + pool_eps)
        pieces.append(leading * factor)
        factors.append(factor)
    pools = lax.all_gather(jnp.concatenate(pieces, axis=1), "dp", axis=0, tiled=True)
    d_pooled = jnp.zeros_like(pooled)
    offset = 0
    for keep_width, factor in zip(truncations(model_width), factors):
        leading = pooled[:, :keep_width]
        upstream = pool_grad[:, offset : offset + keep_width]
        inner = jnp.mean(upstream * leading, axis=1, keepdims=True)
        d_pooled = d_pooled.at[:, :keep_width].add(factor * upstream - leading * factor**3 * inner)
        offset = offset + keep_width
    spread_back = jnp.einsum(
        "st,sd->td", member, d_pooled / denom, precision=highest, preferred_element_type=jnp.float32
    )
    d_final = out_grad.astype(jnp.float32) + spread_back
    g_ffn_part = jnp.sum(d_final * normal_ffn, axis=0)
    b_ffn_part = jnp.sum(d_final, axis=0)
    d_resid = norm_back(d_final * g_ffn, normal_ffn, inverse_ffn)
    b_down_part = jnp.sum(d_resid, axis=0)
    resid_low = d_resid.astype(jnp.bfloat16)
    w_down_part = jnp.einsum("tf,td->fd", act_rows, resid_low, preferred_element_type=jnp.float32)
    d_act = jnp.einsum("td,fd->tf", resid_low, w_down, preferred_element_type=jnp.float32)
    d_upper = jax.vjp(gelu_exact, upper)[1](d_act)[0]
    b_up_part = jnp.sum(d_upper, axis=0)
    upper_low = d_upper.astype(jnp.bfloat16)
    w_up_part = jnp.einsum("td,tf->df", normed_low, upper_low, preferred_element_type=jnp.float32)
    normed_term = jnp.einsum("tf,df->td", upper_low, w_up, preferred_element_type=jnp.float32)
    d_normed = d_resid + lax.psum(normed_term, "tensor")
    g_attn_part = jnp.sum(d_normed * normal_attn, axis=0)
    b_attn_part = jnp.sum(d_normed, axis=0)
    d_hidden = norm_back(d_normed * g_attn, normal_attn, inverse_attn)
    b_out_part = jnp.sum(d_hidden, axis=0)
    hidden_low = d_hidden.astype(jnp.bfloat16)
    w_out_part = jnp.einsum("tc,td->cd", mixed, hidden_low, preferred_element_type=jnp.float32)
    d_mixed = jnp.einsum("td,cd->tc", hidden_low, w_out, preferred_element_type=jnp.float32)
    d_mixed = d_mixed.astype(jnp.bfloat16).reshape(slot_count, head_count, HDIM)
    scores_again = attention_scores(query_heads, key_heads, allowed, score_scale)
    probs = jnp.exp(scores_again - log_total)
    probs_again = probs.astype(jnp.bfloat16)
    d_probs = jnp.einsum("qhd,khd->hqk", d_mixed, value_heads, preferred_element_type=jnp.float32)
    row_inner = jnp.sum(probs * d_probs, axis=-1, keepdims=True)
    d_scores = (probs * (d_probs - row_inner) * score_scale).astype(jnp.bfloat16)
    d_query = jnp.einsum(
        "hqk,khd->qhd", d_scores, key_heads, preferred_element_type=jnp.float32
    ).reshape(slot_count, local_cols)
    d_key = jnp.einsum(
        "hqk,qhd->khd", d_scores, query_heads, preferred_element_type=jnp.float32
    ).reshape(slot_count, local_cols)
    d_value = jnp.einsum(
        "hqk,qhd->khd", probs_again, d_mixed, preferred_element_type=jnp.float32
    ).reshape(slot_count, local_cols)
    b_query_part = jnp.sum(d_query, axis=0)
    b_value_part = jnp.sum(d_value, axis=0)
    query_low = d_query.astype(jnp.bfloat16)
    key_low = d_key.astype(jnp.bfloat16)
    value_low = d_value.astype(jnp.bfloat16)
    w_query_part = jnp.einsum("td,tc->dc", tokens, query_low, preferred_element_type=jnp.float32)
    w_key_part = jnp.einsum("td,tc->dc", tokens, key_low, preferred_element_type=jnp.float32)
    w_value_part = jnp.einsum("td,tc->dc", tokens, value_low, preferred_element_type=jnp.float32)
    input_term = jnp.einsum("tc,dc->td", query_low, w_query, preferred_element_type=jnp.float32)
    input_term = input_term + jnp.einsum(
        "tc,dc->td", key_low, w_key, preferred_element_type=jnp.float32
    )
    input_term = input_term + jnp.einsum(
        "tc,dc->td", value_low, w_value, preferred_element_type=jnp.float32
    )
    d_tokens = d_hidden + lax.psum(input_term, "tensor")
    grad_sums = lax.psum(
        (
            w_query_part,
            w_key_part,
            w_value_part,
            b_query_part,
            b_value_part,
            w_out_part,
            b_out_part,
            g_attn_part,
            b_attn_part,
            w_up_part,
            b_up_part,
            w_down_part,
            b_down_part,
            g_ffn_part,
            b_ffn_part,
        ),
        "dp",
    )
    (
        d_w_query,
        d_w_key,
        d_w_value,
        d_b_query,
        d_b_value,
        d_w_out,
        d_b_out,
        d_g_attn,
        d_b_attn,
        d_w_up,
        d_b_up,
        d_w_down,
        d_b_down,
        d_g_ffn,
        d_b_ffn,
    ) = grad_sums
    return (
        layer_out,
        pools,
        d_tokens,
        d_w_query,
        d_w_key,
        d_w_value,
        d_b_query,
        d_b_value,
        d_w_out,
        d_b_out,
        d_g_attn,
        d_b_attn,
        d_w_up,
        d_b_up,
        d_w_down,
        d_b_down,
        d_g_ffn,
        d_b_ffn,
    )


def solution(mesh):
    return jax.shard_map(
        shards,
        mesh=mesh,
        in_specs=(
            P("dp", None),
            P("dp", None),
            P(None, "tensor"),
            P(None, "tensor"),
            P(None, "tensor"),
            P("tensor"),
            P("tensor"),
            P("tensor", None),
            P(),
            P(),
            P(),
            P(None, "tensor"),
            P("tensor"),
            P("tensor", None),
            P(),
            P(),
            P(),
            P("dp", None),
            P("dp", None),
        ),
        out_specs=(
            P("dp", None),
            P(),
            P("dp", None),
            P(None, "tensor"),
            P(None, "tensor"),
            P(None, "tensor"),
            P("tensor"),
            P("tensor"),
            P("tensor", None),
            P(),
            P(),
            P(),
            P(None, "tensor"),
            P("tensor"),
            P("tensor", None),
            P(),
            P(),
            P(),
        ),
        check_vma=False,
    )
```

profile of v0, /device:TPU:0, one launch (start us, length us, event | category | flops | bytes accessed | tf_op | source)
XLA Modules:
  0.0 486.1 jit_solution(11460330406638272772)
XLA Ops:
  7.3 0.9 copy.49
  8.6 1.7 convolution_convert_fusion.2
  13.3 1.0 convolution_convert_fusion
  14.3 1.6 fusion.70
  16.0 71.8 %all-reduce.8.cloned.1.call-done = f32[512,768]{1,0:T(8,128)} async-done(((f32[512,768]{1,0:T(8,128)}), f32[512,768]{1,0:T(8,128)}) %all-reduce.8.cloned.1.call-update) | async-done | bytes 1572880 | tf_op jit(solution)/shard_map/psum | solution.py:94
  87.7 1.7 fusion.64
  90.2 5.4 %multiply_convert_fusion.1 = (bf16[512,768]{1,0:T(8,128)(2,1)S(1)}, f32[512,768]{1,0:T(8,128)}, f32[512,768]{1,0:T(8,128)}) fusion(f32[768]{0:T(1024)S(1)} %copy-done.59, bf16[768,768]{1,0:T(8,128)(2,1)S(1)} %copy-done, f32[512,768]{1,0:T(8,128)S(1)} %get-tuple-element.189, f32[768]{0:T(1024)S(1)} %copy-done.53, f32[768]{0:T(1024)S(1)} %copy-done.35, ...), kind=kOutput, calls=%fused_computation.24 | convolution fusion | flops 631898112 | bytes 6697984 | tf_op jit(solution)/shard_map/dot_general | solution.py:98
  95.5 0.9 copy-done.16
  96.4 1.9 fusion.71
  99.9 1.2 convert_bitcast_fusion
  101.0 65.6 %all-reduce.10.cloned.1.call-done = f32[512,768]{1,0:T(8,128)} async-done(((f32[512,768]{1,0:T(8,128)}), f32[512,768]{1,0:T(8,128)}) %all-reduce.10.cloned.1.call-update) | async-done | bytes 1572880 | tf_op jit(solution)/shard_map/psum | solution.py:100
  166.7 2.0 fusion.62
  169.7 1.0 multiply_reduce_fusion.9
  173.5 1.3 add_select_fusion.2
  175.5 1.4 scatter-add.19
  177.0 3.9 multiply_reduce_fusion.1
  181.0 1.5 fusion.60
  183.5 1.8 fusion.69
  185.3 0.9 copy-done.63
  186.2 2.0 fusion.42
  188.4 68.0 %all-reduce.12.cloned.1.call-done = f32[512,768]{1,0:T(8,128)} async-done(((f32[512,768]{1,0:T(8,128)}), f32[512,768]{1,0:T(8,128)}) %all-reduce.12.cloned.1.call-update) | async-done | bytes 1572880 | tf_op jit(solution)/shard_map/psum | solution.py:140
  256.4 3.3 multiply_reduce_fusion.2
  259.8 1.1 fusion.61
  260.9 1.1 copy-done.2
  262.5 2.3 fusion.72
  264.8 7.5 %fusion.66 = (f32[3,64]{1,0:T(4,128)}, bf16[512,3,64]{0,2,1:T(8,128)(2,1)S(1)}) fusion(bf16[512,3,64]{0,2,1:T(8,128)(2,1)S(1)} %bitcast.68, f32[3,512,512]{1,2,0:T(8,128)} %fusion.72, f32[3,512]{1,0:T(4,128)S(1)} %copy-done.44, f32[3,512,512]{1,2,0:T(8,128)} %copy-done.8, pred[512,512]{0,1:T(8,128)(4,1)S(1)} %copy-done.12), kind=kOutput, calls=%fused_computation.151 | convolution fusion | flops 109512512 | bytes 6953728 | tf_op jit(solution)/shard_map/hqk,khd->qhd/dot_general | solution.py:155
  272.3 6.9 %fusion.27 = bf16[3,64,512]{2,1,0:T(8,128)(2,1)S(1)} fusion(bf16[512,3,64]{0,2,1:T(8,128)(2,1)} %bitcast.78, f32[3,512,512]{1,2,0:T(8,128)} %fusion.72, f32[3,512,512]{1,2,0:T(8,128)} %copy-done.8, f32[3,512]{1,0:T(4,128)S(1)} %copy-done.44, pred[512,512]{0,1:T(8,128)(4,1)S(1)} %copy-done.12), kind=kOutput, calls=%fused_computation.60 | convolution fusion | flops 109414400 | bytes 6952960 | tf_op jit(solution)/shard_map/hqk,qhd->khd/dot_general | solution.py:158
  279.3 3.6 fusion.65
  284.2 1.6 add_add_fusion
  285.9 3.9 fusion.44
  289.8 2.4 fusion.40
  292.2 1.1 convolution_bitcast_fusion.2
  293.4 1.1 convolution_bitcast_fusion.1
  294.5 1.1 convolution_bitcast_fusion
  295.7 1.1 fusion.37
  297.7 10.6 %all_gather.3 = f32[128,1728]{1,0:T(8,128)S(1)} all-gather(f32[16,1728]{1,0:T(8,128)S(1)} %copy-done.30), channel_id=1, replica_groups=mesh['dp'=8,'tensor'=4] {'dp'}, dimensions={0}, use_global_device_ids=true | all-gather | bytes 995328 | tf_op jit(solution)/shard_map/all_gather | solution.py:115
  308.3 1.2 copy.54
  309.7 25.0 %all-reduce = (f32[192]{0:T(256)}, f32[192]{0:T(256)}, f32[768]{0:T(1024)}, f32[768]{0:T(1024)}, f32[768]{0:T(1024)}, /*index=5*/f32[768]{0:T(1024)}, f32[768]{0:T(1024)}, f32[768]{0:T(1024)}, f32[768]{0:T(1024)}) all-reduce(f32[192]{0:T(256)S(1)} %reduce_sum.296, ...), channel_id=1, replica_groups=mesh['dp'=8,'tensor'=4] {'dp'}, use_global_device_ids=true, to_apply=%region_35.36 | all-reduce | flops 5760 | bytes 46080 | tf_op jit(solution)/shard_map/psum | solution.py:180
  334.7 19.3 %all-reduce.14.cloned.1.call-done = f32[512,768]{1,0:T(8,128)} async-done(((f32[512,768]{1,0:T(8,128)}), f32[512,768]{1,0:T(8,128)}) %all-reduce.14.cloned.1.call-update) | async-done | bytes 1572880 | tf_op jit(solution)/shard_map/psum | solution.py:179
  354.1 2.7 add.261
  356.8 114.3 %all-reduce.16.cloned.1.call-done = (f32[768,192]{0,1:T(8,128)}, f32[768,192]{0,1:T(8,128)}, f32[768,192]{0,1:T(8,128)}, f32[192,768]{1,0:T(8,128)}, f32[768,768]{1,0:T(8,128)}, /*index=5*/f32[768,768]{1,0:T(8,128)}) async-done(((f32[768,192]{0,1:T(8,128)}, f32[768,192]{0,1:T(8,128)}, f32[768,192]{0,1:T(8,128)}, f32[192,768]{1,0:T(8,128)}, f32[768,768]{1,0:T(8,128)}, /*index=5*/f32[768,768]{1,0:T(8,128)}), ...) | async-done | bytes 7077904 | tf_op jit(solution)/shard_map/psum | solution.py:180
  471.1 2.0 copy.77
  473.2 0.8 copy.78
  474.0 0.8 copy.79
  474.8 0.8 copy.80
  475.6 1.4 copy.81
  477.0 1.1 copy-done.9
  478.1 1.4 copy.82
  (179 shorter events, 14.3 us)
Async XLA Ops:
  7.2 82.6 %copy-start = (bf16[768,768]{1,0:T(8,128)(2,1)S(1)}, bf16[768,768]{1,0:T(8,128)(2,1)}, u32[]{:S(2)}) copy-start(bf16[768,768]{1,0:T(8,128)(2,1)} %param.42) | copy-start | bytes 3538948
  7.2 3.1 copy-start.4
  7.2 3.1 copy-start.26
  7.2 3.1 copy-start.60
  7.2 80.5 %all-reduce.8.cloned.1.call-start = ((), (), s32[]{:S(2)}) async-start(), calls=%async_computation | async-start | bytes 3145728 | tf_op jit(solution)/shard_map/psum | solution.py:94
  8.6 4.6 copy-start.11
  11.6 1.7 copy-start.8
  14.3 73.4 %copy-start.52 = (f32[768]{0:T(1024)S(1)}, f32[768]{0:T(1024)}, u32[]{:S(2)}) copy-start(f32[768]{0:T(1024)} %param.39) | copy-start | bytes 9220
  15.9 150.8 %all-reduce.10.cloned.1.call-start = ((), (), s32[]{:S(2)}) async-start(), calls=%async_computation.1 | async-start | bytes 3145728 | tf_op jit(solution)/shard_map/psum | solution.py:100
  90.1 6.3 %copy-start.57 = (bf16[768,768]{1,0:T(8,128)(2,1)S(1)}, bf16[768,768]{1,0:T(8,128)(2,1)}, u32[]{:S(2)}) copy-start(bf16[768,768]{1,0:T(8,128)(2,1)} %param.44) | copy-start | bytes 3538948
  98.4 158.1 %all-reduce.12.cloned.1.call-start = ((), (), s32[]{:S(2)}) async-start(), calls=%async_computation.2 | async-start | bytes 3145728 | tf_op jit(solution)/shard_map/psum | solution.py:140
  168.6 2.1 copy-start.5
  168.7 2.0 copy-start.36
  169.7 5.9 %copy-start.41 = (f32[512]{0:T(512)}, f32[512]{0:T(512)S(1)}, u32[]{:S(2)}) copy-start(f32[512]{0:T(512)S(1)} %add_rsqrt_fusion) | copy-start | bytes 6148
  173.5 2.0 copy-start.34
  176.9 4.0 copy-start.6
  176.9 4.0 copy-start.37
  176.9 4.0 copy-start.42
  176.9 4.0 copy-start.46
  176.9 4.0 copy-start.48
  180.9 2.0 copy-start.65
  180.9 2.6 copy-start.66
  182.5 2.8 copy-start.7
  188.2 165.9 %all-reduce.14.cloned.1.call-start = ((), (), s32[]{:S(2)}) async-start(), calls=%async_computation.3 | async-start | bytes 3145728 | tf_op jit(solution)/shard_map/psum | solution.py:179
  259.8 2.2 copy-start.15
  262.4 2.4 copy-start.12
  262.5 2.3 copy-start.20
  262.5 2.3 copy-start.44
  279.3 3.6 copy-start.27
  285.8 4.0 copy-start.54
  285.8 185.3 %all-reduce.16.cloned.1.call-start = ((), (), s32[]{:S(2)}) async-start(), calls=%async_computation.4 | async-start | bytes 14155776 | tf_op jit(solution)/shard_map/psum | solution.py:180
  285.9 3.9 copy-start.64
  293.4 2.3 copy-start.3
  293.4 2.3 copy-start.18
  296.8 12.7 %copy-start.55 = (f32[3,64]{1,0:T(4,128)S(1)}, f32[3,64]{1,0:T(4,128)}, u32[]{:S(2)}) copy-start(f32[3,64]{1,0:T(4,128)} %get-tuple-element.193) | copy-start | bytes 2308
  296.8 12.8 %copy-start.56 = (f32[3,64]{1,0:T(4,128)S(1)}, f32[3,64]{1,0:T(4,128)}, u32[]{:S(2)}) copy-start(f32[3,64]{1,0:T(4,128)} %get-tuple-element.191) | copy-start | bytes 2308
  296.9 12.9 %copy-start.38 = (f32[768]{0:T(1024)S(1)}, f32[768]{0:T(1024)}, u32[]{:S(2)}) copy-start(f32[768]{0:T(1024)} %get-tuple-element.175) | copy-start | bytes 9220
  296.9 12.8 %copy-start.39 = (f32[768]{0:T(1024)S(1)}, f32[768]{0:T(1024)}, u32[]{:S(2)}) copy-start(f32[768]{0:T(1024)} %get-tuple-element.142) | copy-start | bytes 9220
  296.9 12.8 %copy-start.40 = (f32[768]{0:T(1024)S(1)}, f32[768]{0:T(1024)}, u32[]{:S(2)}) copy-start(f32[768]{0:T(1024)} %get-tuple-element.147) | copy-start | bytes 9220
  296.9 12.8 %copy-start.49 = (f32[768]{0:T(1024)S(1)}, f32[768]{0:T(1024)}, u32[]{:S(2)}) copy-start(f32[768]{0:T(1024)} %get-tuple-element.140) | copy-start | bytes 9220
  296.9 12.8 %copy-start.50 = (f32[768]{0:T(1024)S(1)}, f32[768]{0:T(1024)}, u32[]{:S(2)}) copy-start(f32[768]{0:T(1024)} %get-tuple-element.146) | copy-start | bytes 9220
  296.9 12.8 %copy-start.51 = (f32[768]{0:T(1024)S(1)}, f32[768]{0:T(1024)}, u32[]{:S(2)}) copy-start(f32[768]{0:T(1024)} %get-tuple-element.219) | copy-start | bytes 9220
  471.1 2.1 copy-start.23
  471.1 2.9 copy-start.22
  471.1 3.7 copy-start.21
  473.2 2.5 copy-start.10
  475.6 2.5 copy-start.9
  475.6 3.9 copy-start.1
  (24 other events, 25.5 us)
Sparse Core Ops, SparseCore 0:
  16.0 71.6 all-reduce.7
  98.5 68.1 all-reduce.9
  188.3 68.1 all-reduce.11
  285.9 68.0 all-reduce.13
  359.1 111.9 all-reduce.15
where the time goes:
time: 487 us; the launch traced here: 486 us
  waiting for transfers between devices  339 us (70%)
  matrix products  55.8 us (11%)
  blocking collectives  35.6 us (7%)
  other arithmetic  20.7 us (4%)
  local copies, waits for them, and re-layouts  19.7 us (4%)
  between operations  14.5 us (3%)
    psum x1, waiting for transfers between devices, shards(): lax.psum((w_query_part, w_key_part, w_value_part, b_query_part, b_value_p...  114 us
    psum x1, waiting for transfers between devices, shards(): attn_total = lax.psum(partial_value, 'tensor')  71.8 us
    psum x1, waiting for transfers between devices, shards(): d_normed = d_resid + lax.psum(normed_term, 'tensor')  68 us
    psum x1, waiting for transfers between devices, shards(): lax.psum(jnp.dot(act_rows, w_down, preferred_element_type=jnp.float32), '...  65.6 us
    psum x1, blocking collectives, shards(): lax.psum((w_query_part, w_key_part, w_value_part, b_query_part, b_value_p...  25 us
    psum x1, waiting for transfers between devices, shards(): d_tokens = d_hidden + lax.psum(input_term, 'tensor')  19.3 us
    unnamed x141, local copies, waits for them, and re-layouts  17.3 us
    all_gather x1, blocking collectives, shards(): lax.all_gather(jnp.concatenate(pieces, axis=1), 'dp', axis=0, tiled=True)  10.6 us
  transfers between devices with their start and end apart: 5, of which 5 were waited for; matrix products, arithmetic and copies ran while one was open for 4% of the time, Pallas kernels for 0%

commit v1 on v0

--- a/solution.py
+++ b/solution.py
@@ -91,7 +91,11 @@
     mixed = jnp.einsum("hqk,khd->qhd", probs_low, value_heads, preferred_element_type=jnp.float32)
     mixed = mixed.reshape(slot_count, local_cols).astype(jnp.bfloat16)
     partial_value = jnp.dot(mixed, w_out, preferred_element_type=jnp.float32)
-    attn_total = lax.psum(partial_value, "tensor")
+    attn_total = partial_value
+    for hop in (1, 2):
+        attn_total = attn_total + lax.ppermute(
+            attn_total, "tensor", [(dev, dev ^ hop) for dev in range(4)]
+        )
     normal_attn, inverse_attn = norm_stats(inputs + attn_total + b_out)
     normed = normal_attn * g_attn + b_attn
     normed_low = normed.astype(jnp.bfloat16)

time: 487 us -> 518 us (1.064)
  waiting for transfers between devices: 339 us -> 371 us
  starting transfers between devices: 0.61 us -> 6.5 us
    ppermute x0 -> x2, waiting for transfers between devices: none -> 102 us  [shards(): lax.ppermute(attn_total, 'tensor', [(dev, dev ^ hop) for dev in range(4)])]
    psum x1 -> x0, waiting for transfers between devices: 71.8 us -> none  [shards(): attn_total = lax.psum(partial_value, 'tensor')]
    ppermute x0 -> x2, starting transfers between devices: none -> 5.94 us  [shards(): lax.ppermute(attn_total, 'tensor', [(dev, dev ^ hop) for dev in range(4)])]
    unnamed x141 -> x133, local copies, waits for them, and re-layouts: 17.3 us -> 17.7 us
  transfers between devices with their start and end apart: 5 -> 6, of which waited for: 5 -> 6; matrix products, arithmetic and copies ran while one was open for 4% -> 3% of each run, Pallas kernels for 0% -> 0%
where the time goes in v1:
time: 518 us
  waiting for transfers between devices  371 us (72%)
  matrix products  51.7 us (10%)
  blocking collectives  35.6 us (7%)
  local copies, waits for them, and re-layouts  20.1 us (4%)
  other arithmetic  18.4 us (4%)
  between operations  14.5 us (3%)
  starting transfers between devices  6.5 us (1%)
    psum x1, waiting for transfers between devices, shards(): lax.psum((w_query_part, w_key_part, w_value_part, b_query_part, b_value_p...  114 us
    ppermute x2, waiting for transfers between devices, shards(): lax.ppermute(attn_total, 'tensor', [(dev, dev ^ hop) for dev in range(4)])  102 us
    psum x1, waiting for transfers between devices, shards(): d_normed = d_resid + lax.psum(normed_term, 'tensor')  68 us
    psum x1, waiting for transfers between devices, shards(): lax.psum(jnp.dot(act_rows, w_down, preferred_element_type=jnp.float32), '...  67.5 us
    psum x1, blocking collectives, shards(): lax.psum((w_query_part, w_key_part, w_value_part, b_query_part, b_value_p...  25 us
    psum x1, waiting for transfers between devices, shards(): d_tokens = d_hidden + lax.psum(input_term, 'tensor')  19.4 us
    unnamed x133, local copies, waits for them, and re-layouts  17.7 us
    all_gather x1, blocking collectives, shards(): lax.all_gather(jnp.concatenate(pieces, axis=1), 'dp', axis=0, tiled=True)  10.6 us
  transfers between devices with their start and end apart: 6, of which 6 were waited for; matrix products, arithmetic and copies ran while one was open for 3% of the time, Pallas kernels for 0%

profile of v1, /device:TPU:0, one launch (start us, length us, event | category | flops | bytes accessed | tf_op | source)
XLA Modules:
  0.0 517.9 jit_solution(4581010289319718198)
XLA Ops:
  7.3 0.9 copy.49
  8.6 1.7 convolution_convert_fusion.2
  13.3 1.0 convolution_convert_fusion
  14.7 3.1 collective-permute-start
  17.8 34.4 %collective-permute-done = f32[512,768]{1,0:T(8,128)S(1)} collective-permute-done((f32[512,768]{1,0:T(8,128)S(1)}, f32[512,768]{1,0:T(8,128)S(1)}, u32[]{:S(2)}, u32[]{:S(2)}) %collective-permute-start) | collective-permute-done | bytes 1572896 | tf_op jit(solution)/shard_map/ppermute | solution.py:96
  52.4 2.8 collective-permute-start.1
  55.3 67.4 %collective-permute-done.1 = f32[512,768]{1,0:T(8,128)S(1)} collective-permute-done((f32[512,768]{1,0:T(8,128)S(1)}, f32[512,768]{1,0:T(8,128)S(1)}, u32[]{:S(2)}, u32[]{:S(2)}) %collective-permute-start.1) | collective-permute-done | bytes 1572896 | tf_op jit(solution)/shard_map/ppermute | solution.py:96
  123.8 5.4 %multiply_convert_fusion.1 = (bf16[512,768]{1,0:T(8,128)(2,1)S(1)}, f32[512,768]{1,0:T(8,128)}, f32[512,768]{1,0:T(8,128)}) fusion(f32[768]{0:T(1024)S(1)} %copy-done.55, bf16[768,768]{1,0:T(8,128)(2,1)S(1)} %copy-done, f32[512,768]{1,0:T(8,128)S(1)} %get-tuple-element.189, f32[768]{0:T(1024)S(1)} %copy-done.51, f32[768]{0:T(1024)S(1)} %copy-done.36, ...), kind=kOutput, calls=%fused_computation.24 | convolution fusion | flops 631898112 | bytes 6697984 | tf_op jit(solution)/shard_map/dot_general | solution.py:102
  129.1 0.9 copy-done.17
  130.0 1.9 fusion.71
  133.5 1.2 convert_bitcast_fusion
  134.7 67.5 %all-reduce.7.cloned.1.call-done = f32[512,768]{1,0:T(8,128)} async-done(((f32[512,768]{1,0:T(8,128)}), f32[512,768]{1,0:T(8,128)}) %all-reduce.7.cloned.1.call-update) | async-done | bytes 1572880 | tf_op jit(solution)/shard_map/psum | solution.py:104
  202.1 2.0 fusion.62
  205.2 1.0 multiply_reduce_fusion.9
  209.0 1.3 add_select_fusion.2
  211.0 1.4 scatter-add.19
  212.4 3.9 multiply_reduce_fusion.1
  216.4 1.5 fusion.60
  219.0 1.8 fusion.69
  220.8 0.9 copy-done.59
  221.6 2.0 fusion.42
  223.9 68.0 %all-reduce.9.cloned.1.call-done = f32[512,768]{1,0:T(8,128)} async-done(((f32[512,768]{1,0:T(8,128)}), f32[512,768]{1,0:T(8,128)}) %all-reduce.9.cloned.1.call-update) | async-done | bytes 1572880 | tf_op jit(solution)/shard_map/psum | solution.py:144
  291.9 2.7 multiply_reduce_fusion.2
  296.1 1.2 copy-done.9
  297.3 1.1 fusion.65
  298.3 2.3 fusion.72
  300.7 7.0 %fusion.66 = (f32[3,64]{1,0:T(4,128)S(1)}, bf16[512,3,64]{0,2,1:T(8,128)(2,1)S(1)}) fusion(bf16[512,3,64]{0,2,1:T(8,128)(2,1)S(1)} %bitcast.68, f32[3,512,512]{1,2,0:T(8,128)} %fusion.72, f32[3,512]{1,0:T(4,128)S(1)} %copy-done.42, f32[3,512,512]{1,2,0:T(8,128)} %copy-done.8, pred[512,512]{0,1:T(8,128)(4,1)S(1)} %copy-done.13), kind=kOutput, calls=%fused_computation.151 | convolution fusion | flops 109512512 | bytes 6953728 | tf_op jit(solution)/shard_map/hqk,khd->qhd/dot_general | solution.py:159
  307.6 6.9 %fusion.27 = bf16[3,64,512]{2,1,0:T(8,128)(2,1)S(1)} fusion(bf16[512,3,64]{0,2,1:T(8,128)(2,1)} %bitcast.78, f32[3,512,512]{1,2,0:T(8,128)} %fusion.72, f32[3,512,512]{1,2,0:T(8,128)} %copy-done.8, f32[3,512]{1,0:T(4,128)S(1)} %copy-done.42, pred[512,512]{0,1:T(8,128)(4,1)S(1)} %copy-done.13), kind=kOutput, calls=%fused_computation.60 | convolution fusion | flops 109414400 | bytes 6952960 | tf_op jit(solution)/shard_map/hqk,qhd->khd/dot_general | solution.py:162
  316.0 1.6 add_add_fusion
  317.6 3.9 fusion.44
  321.6 2.4 fusion.40
  324.0 1.1 convolution_bitcast_fusion
  325.1 1.1 convolution_bitcast_fusion.1
  326.3 1.1 convolution_bitcast_fusion.2
  327.4 1.1 fusion.37
  328.6 0.8 copy-done.31
  329.5 10.6 %all_gather.3 = f32[128,1728]{1,0:T(8,128)S(1)} all-gather(f32[16,1728]{1,0:T(8,128)S(1)} %copy-done.31), channel_id=1, replica_groups=mesh['dp'=8,'tensor'=4] {'dp'}, dimensions={0}, use_global_device_ids=true | all-gather | bytes 995328 | tf_op jit(solution)/shard_map/all_gather | solution.py:119
  340.1 1.2 copy.54
  341.5 25.0 %all-reduce = (f32[192]{0:T(256)}, f32[192]{0:T(256)}, f32[768]{0:T(1024)}, f32[768]{0:T(1024)}, f32[768]{0:T(1024)}, /*index=5*/f32[768]{0:T(1024)}, f32[768]{0:T(1024)}, f32[768]{0:T(1024)}, f32[768]{0:T(1024)}) all-reduce(f32[192]{0:T(256)S(1)} %reduce_sum.296, ...), channel_id=1, replica_groups=mesh['dp'=8,'tensor'=4] {'dp'}, use_global_device_ids=true, to_apply=%region_34.35 | all-reduce | flops 5760 | bytes 46080 | tf_op jit(solution)/shard_map/psum | solution.py:184
  366.4 19.4 %all-reduce.11.cloned.1.call-done = f32[512,768]{1,0:T(8,128)} async-done(((f32[512,768]{1,0:T(8,128)}), f32[512,768]{1,0:T(8,128)}) %all-reduce.11.cloned.1.call-update) | async-done | bytes 1572880 | tf_op jit(solution)/shard_map/psum | solution.py:183
  385.8 2.7 add.267
  388.6 114.3 %all-reduce.13.cloned.1.call-done = (f32[768,192]{0,1:T(8,128)}, f32[768,192]{0,1:T(8,128)}, f32[768,192]{0,1:T(8,128)}, f32[192,768]{1,0:T(8,128)}, f32[768,768]{1,0:T(8,128)}, /*index=5*/f32[768,768]{1,0:T(8,128)}) async-done(((f32[768,192]{0,1:T(8,128)}, f32[768,192]{0,1:T(8,128)}, f32[768,192]{0,1:T(8,128)}, f32[192,768]{1,0:T(8,128)}, f32[768,768]{1,0:T(8,128)}, /*index=5*/f32[768,768]{1,0:T(8,128)}), ...) | async-done | bytes 7077904 | tf_op jit(solution)/shard_map/psum | solution.py:184
  502.9 2.0 copy.76
  505.0 0.8 copy.77
  505.8 0.8 copy.78
  507.4 1.4 copy.80
  508.8 1.1 copy-done.10
  509.9 1.4 copy.81
  (173 shorter events, 16.1 us)
Async XLA Ops:
  7.2 116.2 %copy-start = (bf16[768,768]{1,0:T(8,128)(2,1)S(1)}, bf16[768,768]{1,0:T(8,128)(2,1)}, u32[]{:S(2)}) copy-start(bf16[768,768]{1,0:T(8,128)(2,1)} %param.42) | copy-start | bytes 3538948
  7.2 3.1 copy-start.4
  7.2 3.1 copy-start.27
  7.2 3.1 copy-start.56
  7.2 194.9 %all-reduce.7.cloned.1.call-start = ((), (), s32[]{:S(2)}) async-start(), calls=%async_computation | async-start | bytes 3145728 | tf_op jit(solution)/shard_map/psum | solution.py:104
  8.6 4.6 copy-start.12
  11.6 1.7 copy-start.8
  12.8 1.5 copy-start.41
  14.3 3.6 copy-start.18
  14.7 108.0 %copy-start.50 = (f32[768]{0:T(1024)S(1)}, f32[768]{0:T(1024)}, u32[]{:S(2)}) copy-start(f32[768]{0:T(1024)} %param.39) | copy-start | bytes 9220
  14.7 37.5 %collective-permute-start = (f32[512,768]{1,0:T(8,128)S(1)}, f32[512,768]{1,0:T(8,128)S(1)}, u32[]{:S(2)}, u32[]{:S(2)}) collective-permute-start(f32[512,768]{1,0:T(8,128)S(1)} %fusion.70), channel_id=1, source_target_pairs={{0,1},{1,0},{2,3},{3,2},{4,5},{5,4},{6,7},{7,6},{8,9},{9,8},{10,11... | collective-permute-start | bytes 4718600 | tf_op jit(solution)/shard_map/ppermute | solution.py:96
  52.4 70.2 %collective-permute-start.1 = (f32[512,768]{1,0:T(8,128)S(1)}, f32[512,768]{1,0:T(8,128)S(1)}, u32[]{:S(2)}, u32[]{:S(2)}) collective-permute-start(f32[512,768]{1,0:T(8,128)S(1)} %add.238), channel_id=1, source_target_pairs={{0,2},{1,3},{2,0},{3,1},{4,6},{5,7},{6,4},{7,5},{8,10},{9,11},{10,... | collective-permute-start | bytes 4718600 | tf_op jit(solution)/shard_map/ppermute | solution.py:96
  123.8 6.3 %copy-start.53 = (bf16[768,768]{1,0:T(8,128)(2,1)S(1)}, bf16[768,768]{1,0:T(8,128)(2,1)}, u32[]{:S(2)}) copy-start(bf16[768,768]{1,0:T(8,128)(2,1)} %param.44) | copy-start | bytes 3538948
  132.0 159.9 %all-reduce.9.cloned.1.call-start = ((), (), s32[]{:S(2)}) async-start(), calls=%async_computation.1 | async-start | bytes 3145728 | tf_op jit(solution)/shard_map/psum | solution.py:144
  204.1 2.1 copy-start.5
  204.2 2.0 copy-start.37
  205.1 5.9 %copy-start.39 = (f32[512]{0:T(512)}, f32[512]{0:T(512)S(1)}, u32[]{:S(2)}) copy-start(f32[512]{0:T(512)S(1)} %add_rsqrt_fusion) | copy-start | bytes 6148
  209.0 2.0 copy-start.35
  212.4 4.0 copy-start.6
  212.4 4.0 copy-start.38
  212.4 4.0 copy-start.40
  212.4 4.0 copy-start.44
  212.4 4.0 copy-start.46
  216.4 1.6 copy-start.54
  216.4 2.0 copy-start.61
  216.4 2.6 copy-start.62
  217.9 2.8 copy-start.7
  223.6 162.2 %all-reduce.11.cloned.1.call-start = ((), (), s32[]{:S(2)}) async-start(), calls=%async_computation.2 | async-start | bytes 3145728 | tf_op jit(solution)/shard_map/psum | solution.py:183
  294.7 2.6 copy-start.9
  295.2 3.1 copy-start.2
  295.2 2.0 copy-start.13
  295.2 2.0 copy-start.42
  298.3 2.3 copy-start.21
  307.6 7.0 %copy-start.14 = (bf16[768,192]{0,1:T(8,128)(2,1)S(1)}, bf16[768,192]{0,1:T(8,128)(2,1)}, u32[]{:S(2)}) copy-start(bf16[768,192]{0,1:T(8,128)(2,1)} %param.34) | copy-start | bytes 884740
  317.6 4.0 copy-start.52
  317.6 185.3 %all-reduce.13.cloned.1.call-start = ((), (), s32[]{:S(2)}) async-start(), calls=%async_computation.3 | async-start | bytes 14155776 | tf_op jit(solution)/shard_map/psum | solution.py:184
  317.6 3.9 copy-start.60
  325.1 2.3 copy-start.3
  325.1 2.3 copy-start.19
  328.6 12.9 %copy-start.47 = (f32[768]{0:T(1024)S(1)}, f32[768]{0:T(1024)}, u32[]{:S(2)}) copy-start(f32[768]{0:T(1024)} %get-tuple-element.140) | copy-start | bytes 9220
  328.6 12.9 %copy-start.48 = (f32[768]{0:T(1024)S(1)}, f32[768]{0:T(1024)}, u32[]{:S(2)}) copy-start(f32[768]{0:T(1024)} %get-tuple-element.146) | copy-start | bytes 9220
  328.6 12.9 %copy-start.49 = (f32[768]{0:T(1024)S(1)}, f32[768]{0:T(1024)}, u32[]{:S(2)}) copy-start(f32[768]{0:T(1024)} %get-tuple-element.219) | copy-start | bytes 9220
  502.9 2.1 copy-start.24
  502.9 2.9 copy-start.23
  502.9 3.7 copy-start.22
  504.9 2.5 copy-start.11
  507.4 2.5 copy-start.10
  507.4 3.9 copy-start.1
  (21 other events, 20.2 us)
Sparse Core Ops, SparseCore 0:
  132.1 69.9 all-reduce.6
  223.8 68.1 all-reduce.8
  317.7 68.1 all-reduce.10
  390.9 111.9 all-reduce.12
